TPU v7x, 32 devices: a whole 2x2x4 slice. The times are simulated.
32 devices in a mesh: row: 2 (over x), col: 4 (over z), freq: 4 (over y, core).
Axes of the slice: x: 2, y: 2, z: 4, core: 2. Of those that a mesh axis runs over, the one named last changes fastest.
Arguments:
- data: bfloat16 [2, 4, 2048, 2048], P(None, 'freq', 'row', 'col'), may hold values from -4.7729708 to 4.7729708, as said below
- primaries: bfloat16 [2, 4, 2048, 2048], P(None, 'freq', 'row', 'col'), may hold values from -6 to 6
Outputs:
- updated_primaries: bfloat16 [2, 4, 2048, 2048], P(None, 'freq', 'row', 'col')
- updated_residual: float32 [2, 4, 2048, 2048], P(None, 'freq', 'row', 'col')
Inputs may be any that keep to these rules, and one draw needn't show every extreme that they name: `data`: magnitudes vary by source, receiver and frequency.
All inputs are finite; a program needn't handle non-finite values.
Results may differ from a plain program's by a relative error of at most 0.0045.
Values may be sent and summed in bfloat16 or wider, within the bound.
No kernel may reach another device: no remote copies, remote signals or barrier semaphores. Data moves between devices by JAX's collectives and lax.ppermute only.
A program may use at most 128 MiB of HBM per device.

v0:
```python
import jax
import jax.numpy as jnp
from jax import lax
from jax.sharding import PartitionSpec as P


def batched(left, right):
    return jnp.einsum("fik,fkj->fij", left, right, preferred_element_type=jnp.float32)


def complex_product(left, right):
    real = batched(left[0], right[0]) - batched(left[1], right[1])
    imag = batched(left[0], right[1]) + batched(left[1], right[0])
    return jnp.stack([real, imag])


def gradient_step(data_part, primary_part):
    src_rows = data_part.shape[2]
    columns = lax.all_gather(data_part, "row", axis=2, tiled=True)

    def add_block(piece):
        return complex_product(piece, columns)

    forward = add_block(lax.all_gather(primary_part, "col", axis=3, tiled=True))
    residual = data_part.astype(jnp.float32) - primary_part.astype(jnp.float32) + forward
    rounded = residual.astype(jnp.bfloat16)
    real = jnp.einsum("fjk,fik->jfi", columns[0], rounded[0], preferred_element_type=jnp.float32)
    real = real + jnp.einsum(
        "fjk,fik->jfi", columns[1], rounded[1], preferred_element_type=jnp.float32
    )
    imag = jnp.einsum("fjk,fik->jfi", columns[0], rounded[1], preferred_element_type=jnp.float32)
    imag = imag - jnp.einsum(
        "fjk,fik->jfi", columns[1], rounded[0], preferred_element_type=jnp.float32
    )
    summed = lax.psum_scatter(
        jnp.concatenate([real, imag], axis=2), "col", scatter_dimension=0, tiled=True
    )
    adjoint = jnp.stack([summed[:, :, :src_rows], summed[:, :, src_rows:]]).transpose(0, 2, 3, 1)
    gradient = (adjoint - residual).astype(jnp.bfloat16)
    moved = add_block(lax.all_gather(gradient, "col", axis=3, tiled=True))
    change = moved - gradient.astype(jnp.float32)
    return (residual, gradient, change)


def local(data, primaries):
    res, grad, chg = gradient_step(data, primaries)
    inner_local = jnp.sum(chg * res)
    energy_local = jnp.sum(chg * chg)
    inner, energy = lax.psum((inner_local, energy_local), ("row", "col", "freq"))
    step = -inner / (energy + 1e-06)
    updated_primaries = (primaries.astype(jnp.float32) + step * grad.astype(jnp.float32)).astype(
        jnp.bfloat16
    )
    updated_residual = res + step * chg
    return (updated_primaries, updated_residual)


def solution(mesh):
    in_specs = (P(None, "freq", "row", "col"), P(None, "freq", "row", "col"))
    out_specs = (P(None, "freq", "row", "col"), P(None, "freq", "row", "col"))
    return jax.shard_map(local, mesh=mesh, in_specs=in_specs, out_specs=out_specs, check_vma=False)
```

profile of v0, /device:TPU:12, one launch (start us, length us, event | category | flops | bytes accessed | tf_op | source)
XLA Modules:
  0.0 759.2 jit_solution(8041567438124025095)
XLA Ops:
  7.2 0.7 all-gather.6.cloned.1.call-update
  7.9 0.7 all-gather.4.cloned.1.call-update
  8.6 0.0 reduce-scatter.2.cloned.1.call-start
  8.7 58.7 %all-gather.6.cloned.1.call-done = bf16[2,1,2048,512]{3,2,1,0:T(8,128)(2,1)} async-done(((bf16[2,1,1024,512]{3,2,1,0:T(8,128)(2,1)}), bf16[2,1,2048,512]{3,2,1,0:T(8,128)(2,1)}) %all-gather.6.cloned.1.call-update) | async-done | bytes 4194320 | tf_op jit(solution)/shard_map/all_gather | solution.py:19
  67.4 148.5 %all-gather.4.cloned.1.call-done = bf16[2,1,1024,2048]{3,2,1,0:T(8,128)(2,1)} async-done(((bf16[2,1,1024,512]{3,2,1,0:T(8,128)(2,1)}), bf16[2,1,1024,2048]{3,2,1,0:T(8,128)(2,1)}) %all-gather.4.cloned.1.call-update) | async-done | bytes 8388624 | tf_op jit(solution)/shard_map/all_gather | solution.py:24
  215.9 5.3 fusion.4
  221.3 1.1 copy-done.10
  222.4 2.3 fusion.5
  224.7 2.3 add_bitcast_fusion.2
  227.1 2.3 subtract_bitcast_fusion.2
  229.4 3.1 fusion.14
  232.5 2.4 fusion.13
  234.8 2.4 fusion.12
  237.2 2.4 subtract_bitcast_fusion
  239.6 2.5 add_bitcast_fusion
  242.1 6.2 pad_maximum_fusion
  248.4 0.0 all-gather.8.cloned.1.call-start
  248.4 278.6 %reduce-scatter.2.cloned.1.call-done = f32[512,1,2048]{0,2,1:T(8,128)} async-done(((f32[2048,1,2048]{0,2,1:T(8,128)}), f32[512,1,2048]{0,2,1:T(8,128)}) %reduce-scatter.2.cloned.1.call-update) | async-done | bytes 4194320 | tf_op jit(solution)/shard_map/reduce_scatter | solution.py:35
  527.0 2.8 slice_bitcast_fusion.13
  529.8 1.4 copy-done.2
  531.2 2.2 fusion.3
  533.4 150.5 %all-gather.8.cloned.1.call-done = bf16[2,1,1024,2048]{3,2,1,0:T(8,128)(2,1)} async-done(((bf16[2,1,1024,512]{3,2,1,0:T(8,128)(2,1)}), bf16[2,1,1024,2048]{3,2,1,0:T(8,128)(2,1)}) %all-gather.8.cloned.1.call-update) | async-done | bytes 8388624 | tf_op jit(solution)/shard_map/all_gather | solution.py:40
  684.0 5.3 fusion.8
  689.3 1.1 copy-done.11
  690.4 2.3 fusion.9
  692.7 2.3 add_bitcast_fusion.1
  695.1 2.3 subtract_bitcast_fusion.1
  697.4 0.6 copy-done.1
  698.0 0.7 copy-done.3
  698.7 2.3 multiply_reduce_fusion
  700.9 43.2 %all-reduce = (f32[]{:T(128)}, f32[]{:T(128)}) all-reduce(f32[]{:T(128)} %get-tuple-element.3, f32[]{:T(128)} %get-tuple-element.2), channel_id=1, replica_groups=mesh['row'=2,'col'=4,'freq'=4] {'row','col','freq'}, use_global_device_ids=true, to_apply=%region_2.0 | all-reduce | flops 2 | bytes 16 | tf_op jit(solution)/shard_map/psum | solution.py:49
  745.5 7.2 multiply_add_fusion
  (23 shorter events, 0.2 us)
Async XLA Ops:
  7.2 60.3 %all-gather.6.cloned.1.call-start = ((), (), s32[]{:S(2)}) async-start(), calls=%async_computation.2 | async-start | bytes 6291456 | tf_op jit(solution)/shard_map/all_gather | solution.py:19
  7.9 208.0 %all-gather.4.cloned.1.call-start = ((), (), s32[]{:S(2)}) async-start(), calls=%async_computation.1 | async-start | bytes 10485760 | tf_op jit(solution)/shard_map/all_gather | solution.py:24
  8.6 518.3 %reduce-scatter.2.cloned.1.call-start = ((), (), s32[]{:S(2)}) async-start(), calls=%async_computation.3 | async-start | bytes 20971520 | tf_op jit(solution)/shard_map/reduce_scatter | solution.py:35
  215.9 5.4 copy-start.8
  215.9 6.4 copy-start.10
  227.0 2.4 copy-start.4
  227.0 2.4 copy-start.7
  248.4 435.6 %all-gather.8.cloned.1.call-start = ((), (), s32[]{:S(2)}) async-start(), calls=%async_computation.4 | async-start | bytes 10485760 | tf_op jit(solution)/shard_map/all_gather | solution.py:40
  527.0 4.2 copy-start
  529.8 1.4 copy-start.2
  684.0 5.3 copy-start.9
  684.0 6.4 copy-start.11
  695.1 2.4 copy-start.5
  695.1 2.9 copy-start.1
  695.1 3.6 copy-start.3
  698.7 2.3 copy-start.6
Sparse Core Ops, SparseCore 0:
  9.5 57.8 all-gather.5
  69.0 146.8 all-gather.3
  248.5 278.4 reduce-scatter.1
  533.5 150.3 all-gather.7
where the time goes:
time: 760 us; the launch traced here: 759 us
  waiting for transfers between devices  638 us (84%)
  blocking collectives  43.2 us (6%)
  matrix products  34.3 us (5%)
  other arithmetic  20.9 us (3%)
  between operations  15.2 us (2%)
  local copies, waits for them, and re-layouts  7.68 us (1%)
    reduce_scatter x1, waiting for transfers between devices, gradient_step(): lax.psum_scatter(jnp.concatenate([real, imag], axis=2), 'col', scatter_di...  279 us
    all_gather x1, waiting for transfers between devices, gradient_step(): moved = add_block(lax.all_gather(gradient, 'col', axis=3, tiled=True))  151 us
    all_gather x1, waiting for transfers between devices, gradient_step(): forward = add_block(lax.all_gather(primary_part, 'col', axis=3, tiled=True))  148 us
    all_gather x1, waiting for transfers between devices, gradient_step(): columns = lax.all_gather(data_part, 'row', axis=2, tiled=True)  58.7 us
    psum x1, blocking collectives, local(): lax.psum((inner_local, energy_local), ('row', 'col', 'freq'))  43.2 us
    dot_general x8, matrix products, batched(): jnp.einsum('fik,fkj->fij', left, right, preferred_element_type=jnp.float32)  24.6 us
  transfers between devices with their start and end apart: 4, of which 4 were waited for; matrix products, arithmetic and copies ran while one was open for 0% of the time, Pallas kernels for 0%

commit v1 on v0

--- a/solution.py
+++ b/solution.py
@@ -1,7 +1,37 @@
+import functools
 import jax
 import jax.numpy as jnp
 from jax import lax
 from jax.sharding import PartitionSpec as P
+from jax.lax import axis_index, axis_size, ppermute
+
+
+def _edit_grid(vals, mesh_dim):
+    f_next = axis_size(mesh_dim)
+    e_now, value_now, all_values = (f_next, axis_index(mesh_dim), vals.shape[3])
+    current_value = map(lambda s: (s, (s + 1) % e_now), range(e_now))
+    copies = list(current_value)
+    out_arr = range(e_now)
+    reached = map(lambda s: (s, (s - 1) % e_now), out_arr)
+    grid = list(reached)
+    b_next = jnp.zeros((*vals.shape[:3], e_now * all_values, *vals.shape[4:]), vals.dtype)
+    b_next = lax.dynamic_update_slice_in_dim(b_next, vals, value_now * all_values, axis=3)
+    part_next = carry_in = vals
+    y1 = e_now // 2
+    for m in range(1, y1 + 1):
+        part_next = ppermute(part_next, axis_name=mesh_dim, perm=copies)
+        b_next = lax.dynamic_update_slice_in_dim(
+            b_next, part_next, (value_now - m) % e_now * all_values, axis=3
+        )
+        if m < e_now - y1:
+            carry_in = ppermute(carry_in, mesh_dim, perm=grid)
+            b_next = lax.dynamic_update_slice_in_dim(
+                b_next, carry_in, (value_now + m) % e_now * all_values, axis=3
+            )
+    return b_next
+
+
+_move_halves = functools.partial(_edit_grid, mesh_dim="col")
 
 
 def batched(left, right):
@@ -37,7 +67,7 @@
     )
     adjoint = jnp.stack([summed[:, :, :src_rows], summed[:, :, src_rows:]]).transpose(0, 2, 3, 1)
     gradient = (adjoint - residual).astype(jnp.bfloat16)
-    moved = add_block(lax.all_gather(gradient, "col", axis=3, tiled=True))
+    moved = add_block(_move_halves(gradient))
     change = moved - gradient.astype(jnp.float32)
     return (residual, gradient, change)
 

time: 760 us -> 765 us (level)
  waiting for transfers between devices: 638 us -> 615 us
  local copies, waits for them, and re-layouts: 7.68 us -> 19.4 us
    all_gather x1 -> x0, waiting for transfers between devices: 151 us -> none  [gradient_step(): moved = add_block(lax.all_gather(gradient, 'col', axis=3, tiled=True))]
    ppermute x0 -> x3, waiting for transfers between devices: none -> 128 us  [the longest x2 128 us: _edit_grid(): part_next = ppermute(part_next, axis_name=mesh_dim, perm=copies)]
    dynamic_update_slice x0 -> x3, local copies, waits for them, and re-layouts: none -> 9.6 us  [the longest x2 6.27 us: _edit_grid(): lax.dynamic_update_slice_in_dim(b_next, part_next, (value_now - m) % e_no...]
  transfers between devices with their start and end apart: 4 -> 6, of which waited for: 4 -> 5; matrix products, arithmetic and copies ran while one was open for 0% -> 1% of each run, Pallas kernels for 0% -> 0%
where the time goes in v1:
time: 765 us; the launch traced here: 763 us
  waiting for transfers between devices  615 us (80%)
  blocking collectives  41.4 us (5%)
  matrix products  40.2 us (5%)
  other arithmetic  23.9 us (3%)
  local copies, waits for them, and re-layouts  19.4 us (3%)
  between operations  15.2 us (2%)
    reduce_scatter x1, waiting for transfers between devices, gradient_step(): lax.psum_scatter(jnp.concatenate([real, imag], axis=2), 'col', scatter_di...  279 us
    all_gather x1, waiting for transfers between devices, gradient_step(): forward = add_block(lax.all_gather(primary_part, 'col', axis=3, tiled=True))  148 us
    ppermute x2, waiting for transfers between devices, _edit_grid(): part_next = ppermute(part_next, axis_name=mesh_dim, perm=copies)  128 us
    all_gather x1, waiting for transfers between devices, gradient_step(): columns = lax.all_gather(data_part, 'row', axis=2, tiled=True)  58.7 us
    psum x1, blocking collectives, local(): lax.psum((inner_local, energy_local), ('row', 'col', 'freq'))  41.4 us
    dot_general x8, matrix products, batched(): jnp.einsum('fik,fkj->fij', left, right, preferred_element_type=jnp.float32)  23.9 us
  transfers between devices with their start and end apart: 6, of which 5 were waited for; matrix products, arithmetic and copies ran while one was open for 1% of the time, Pallas kernels for 0%

profile of v1, /device:TPU:12, one launch (start us, length us, event | category | flops | bytes accessed | tf_op | source)
XLA Modules:
  0.0 763.0 jit_solution(1457570835469894639)
XLA Ops:
  8.7 58.7 %all-gather.5.cloned.1.call-done = bf16[2,1,2048,512]{3,2,1,0:T(8,128)(2,1)} async-done(((bf16[2,1,1024,512]{3,2,1,0:T(8,128)(2,1)}), bf16[2,1,2048,512]{3,2,1,0:T(8,128)(2,1)}) %all-gather.5.cloned.1.call-update) | async-done | bytes 4194320 | tf_op jit(solution)/shard_map/all_gather | solution.py:49
  67.4 148.5 %all-gather.3.cloned.1.call-done = bf16[2,1,1024,2048]{3,2,1,0:T(8,128)(2,1)} async-done(((bf16[2,1,1024,512]{3,2,1,0:T(8,128)(2,1)}), bf16[2,1,1024,2048]{3,2,1,0:T(8,128)(2,1)}) %all-gather.3.cloned.1.call-update) | async-done | bytes 8388624 | tf_op jit(solution)/shard_map/all_gather | solution.py:54
  215.9 5.3 fusion.5
  221.3 1.1 copy-done.9
  222.4 2.3 fusion.4
  224.7 2.3 subtract_bitcast_fusion.2
  227.1 2.3 add_bitcast_fusion.2
  229.4 3.1 fusion.15
  232.5 2.4 fusion.12
  234.8 5.6 fusion.13
  240.4 2.4 add_bitcast_fusion
  242.8 5.9 subtract_bitcast_fusion
  248.7 6.2 pad_maximum_fusion
  255.0 278.6 %reduce-scatter.2.cloned.1.call-done = f32[512,1,2048]{0,2,1:T(8,128)} async-done(((f32[2048,1,2048]{0,2,1:T(8,128)}), f32[512,1,2048]{0,2,1:T(8,128)}) %reduce-scatter.2.cloned.1.call-update) | async-done | bytes 4194320 | tf_op jit(solution)/shard_map/reduce_scatter | solution.py:65
  533.6 2.7 slice_bitcast_fusion.13
  537.3 1.1 copy-done
  538.5 2.3 constant_dynamic-update-slice_fusion.3
  540.8 3.2 copy-done.4
  544.0 5.0 collective-permute-start
  549.0 90.2 %collective-permute-done = bf16[2,1,1024,512]{3,2,1,0:T(8,128)(2,1)} collective-permute-done((bf16[2,1,1024,512]{3,2,1,0:T(8,128)(2,1)}, bf16[2,1,1024,512]{3,2,1,0:T(8,128)(2,1)}, u32[]{:S(2)}, u32[]{:S(2)}) %collective-permute-start) | collective-permute-done | bytes 2097184 | tf_op jit(solution)/shard_map/ppermute | solution.py:22
  639.2 2.5 collective-permute-start.2
  641.7 3.2 constant_dynamic-update-slice_fusion.2
  644.9 3.3 constant_dynamic-update-slice_fusion.1
  648.2 37.9 %collective-permute-done.2 = bf16[2,1,1024,512]{3,2,1,0:T(8,128)(2,1)} collective-permute-done((bf16[2,1,1024,512]{3,2,1,0:T(8,128)(2,1)}, bf16[2,1,1024,512]{3,2,1,0:T(8,128)(2,1)}, u32[]{:S(2)}, u32[]{:S(2)}) %collective-permute-start.2) | collective-permute-done | bytes 2097184 | tf_op jit(solution)/shard_map/ppermute | solution.py:22
  686.1 3.1 constant_dynamic-update-slice_fusion
  689.1 4.7 fusion.11
  693.8 2.3 fusion.10
  696.1 2.3 subtract_bitcast_fusion.1
  698.5 2.3 add_bitcast_fusion.1
  701.4 4.2 multiply_reduce_fusion
  705.6 41.4 %all-reduce = (f32[]{:T(128)}, f32[]{:T(128)}) all-reduce(f32[]{:T(128)} %get-tuple-element.3, f32[]{:T(128)} %get-tuple-element.2), channel_id=1, replica_groups=mesh['row'=2,'col'=4,'freq'=4] {'row','col','freq'}, use_global_device_ids=true, to_apply=%region_2.3 | all-reduce | flops 2 | bytes 16 | tf_op jit(solution)/shard_map/psum | solution.py:79
  748.3 8.1 %multiply_add_fusion = (f32[2,1,1024,512]{3,2,1,0:T(8,128)}, bf16[2,1,1024,512]{3,2,1,0:T(8,128)(2,1)}) fusion(f32[2,1,1024,512]{3,2,1,0:T(8,128)} %get-tuple-element.9, f32[]{:T(128)S(6)} %div.3, bf16[2,1,1024,512]{3,2,1,0:T(8,128)(2,1)} %get-tuple-element.7, f32[1,1,1024,512]{3,2,1,0:T(8,128)} %copy-done.7, f32[1,1,1024,512]{3,2,1,0:T(8,128)} %copy-done.6, ...), kind=kLoop, calls=%fused_computation.16 | loop fusion | flops 9437184 | bytes 18874372 | tf_op jit(solution)/shard_map/add | solution.py:84
  (28 shorter events, 3.2 us)
Async XLA Ops:
  7.2 60.3 %all-gather.5.cloned.1.call-start = ((), (), s32[]{:S(2)}) async-start(), calls=%async_computation.2 | async-start | bytes 6291456 | tf_op jit(solution)/shard_map/all_gather | solution.py:49
  7.9 208.0 %all-gather.3.cloned.1.call-start = ((), (), s32[]{:S(2)}) async-start(), calls=%async_computation.1 | async-start | bytes 10485760 | tf_op jit(solution)/shard_map/all_gather | solution.py:54
  8.6 525.0 %reduce-scatter.2.cloned.1.call-start = ((), (), s32[]{:S(2)}) async-start(), calls=%async_computation.3 | async-start | bytes 20971520 | tf_op jit(solution)/shard_map/reduce_scatter | solution.py:65
  215.9 5.4 copy-start.8
  215.9 6.4 copy-start.9
  227.0 2.4 copy-start.2
  227.0 2.4 copy-start.3
  536.3 2.2 copy-start
  540.8 3.2 copy-start.4
  544.0 95.2 %collective-permute-start = (bf16[2,1,1024,512]{3,2,1,0:T(8,128)(2,1)}, bf16[2,1,1024,512]{3,2,1,0:T(8,128)(2,1)}, u32[]{:S(2)}, u32[]{:S(2)}) collective-permute-start(bf16[2,1,1024,512]{3,2,1,0:T(8,128)(2,1)} %get-tuple-element.7), channel_id=1, source_target_pairs={{0,4},{4,8},{8,12},{12,0},{1,5},{5,9},{9,13},{13,1},{2,6},{6,10},{... | collective-permute-start | bytes 6291464 | tf_op jit(solution)/shard_map/ppermute | solution.py:22
  549.0 95.9 %collective-permute-start.1 = (bf16[2,1,1024,512]{3,2,1,0:T(8,128)(2,1)}, bf16[2,1,1024,512]{3,2,1,0:T(8,128)(2,1)}, u32[]{:S(2)}, u32[]{:S(2)}) collective-permute-start(bf16[2,1,1024,512]{3,2,1,0:T(8,128)(2,1)} %get-tuple-element.7), channel_id=1, source_target_pairs={{0,12},{4,0},{8,4},{12,8},{1,13},{5,1},{9,5},{13,9},{2,14},{6,2},{... | collective-permute-start | bytes 6291464 | tf_op jit(solution)/shard_map/ppermute | solution.py:27
  639.2 46.9 %collective-permute-start.2 = (bf16[2,1,1024,512]{3,2,1,0:T(8,128)(2,1)}, bf16[2,1,1024,512]{3,2,1,0:T(8,128)(2,1)}, u32[]{:S(2)}, u32[]{:S(2)}) collective-permute-start(bf16[2,1,1024,512]{3,2,1,0:T(8,128)(2,1)} %collective-permute-done), channel_id=1, source_target_pairs={{0,4},{4,8},{8,12},{12,0},{1,5},{5,9},{9,13},{13,1},{2,6},{6,10},{... | collective-permute-start | bytes 6291464 | tf_op jit(solution)/shard_map/ppermute | solution.py:22
  644.9 44.3 %copy-start.10 = (bf16[2,1,2048,512]{3,2,1,0:T(8,128)(2,1)S(1)}, bf16[2,1,2048,512]{3,2,1,0:T(8,128)(2,1)}, u32[]{:S(2)}) copy-start(bf16[2,1,2048,512]{3,2,1,0:T(8,128)(2,1)} %all-gather.5.cloned.1.call-done) | copy-start | bytes 12582916
  689.1 4.7 copy-start.5
  698.5 2.4 copy-start.6
  698.5 2.9 copy-start.1
  701.4 4.2 copy-start.7
Sparse Core Ops, SparseCore 0:
  9.5 57.8 all-gather.4
  69.0 146.8 all-gather.2
  255.1 278.4 reduce-scatter.1
